TPU v7x, 256 devices: a whole 4x4x8 slice. The times are simulated.
256 devices in a mesh: frame: 16 (over z_hi, y), space: 16 (over z_lo, x, core).
Axes of the slice: x: 4, y: 4, z: 8 (z_hi: 4, z_lo: 2; z = z_hi * 2 + z_lo), core: 2. Of those that a mesh axis runs over, the one named last changes fastest.
Arguments:
- hidden_in: bfloat16 [2, 16, 32, 64, 1152], P(None, 'frame', 'space'), may hold values from -6 to 6
- attn_cotangent: bfloat16 [2, 16, 32, 64, 1152], P(None, 'frame', 'space'), may hold values from -6 to 6
- w_qkv: bfloat16 [1152, 3456], P('space'), may hold values from -0.1875 to 0.1875
- modulation_table: bfloat16 [1000, 2, 1152], replicated, may hold values from -3 to 3
- snr_table: float32 [1000], replicated, may hold values from 0.1 to 1
- timestep: int32 [2], replicated, may hold values from 0 to 999
- weight_index: int32 [2], replicated, may hold values from 0 to 999
Outputs:
- grad_input: bfloat16 [2, 16, 32, 64, 1152], P(None, 'frame', 'space')
- grad_w_qkv: float32 [1152, 3456], P('space')
- grad_modulation: float32 [2, 2, 1152], replicated
All inputs are finite; a program needn't handle non-finite values.
Results may differ from a plain program's by a relative error of at most 0.029.
Values may be sent and summed in bfloat16 or wider, within the bound.
A program may use at most 128 MiB of HBM per device.

v0:
```python
import jax
import jax.numpy as jnp
from jax import lax
from jax.sharding import PartitionSpec as P

HEADS = 16
HEAD_DIM = 72


def attend_back(queries, keys, values, upstream):
    factor = queries.shape[-1] ** (-0.5)
    queries = queries.astype(jnp.float32)
    keys = keys.astype(jnp.float32)
    values = values.astype(jnp.float32)
    upstream = upstream.astype(jnp.float32)
    highest = lax.Precision.HIGHEST
    scores = jnp.einsum("bfxhe,bgxhe->bxhfg", queries, keys, precision=highest) * factor
    expd = jnp.exp(scores)
    probs = expd / jnp.sum(expd, axis=-1, keepdims=True)
    grad_probs = jnp.einsum("bfxhe,bgxhe->bxhfg", upstream, values, precision=highest)
    grad_values = jnp.einsum("bxhfg,bfxhe->bgxhe", probs, upstream, precision=highest)
    grad_scores = probs * (grad_probs - jnp.sum(probs * grad_probs, axis=-1, keepdims=True))
    grad_queries = jnp.einsum("bxhfg,bgxhe->bfxhe", grad_scores, keys, precision=highest) * factor
    grad_keys = jnp.einsum("bxhfg,bfxhe->bgxhe", grad_scores, queries, precision=highest) * factor
    return (
        grad_queries.astype(jnp.bfloat16),
        grad_keys.astype(jnp.bfloat16),
        grad_values.astype(jnp.bfloat16),
    )


def per_device(
    hidden_in, attn_cotangent, w_qkv, modulation_table, snr_table, timestep, weight_index
):
    clip_count, frame_dev, row_dev, col_count, model_width = hidden_in.shape
    frame_n = lax.axis_size("frame")
    space_n = lax.axis_size("space")
    positions = row_dev * col_count
    w_full = lax.all_gather(w_qkv, "space", axis=0, tiled=True)
    both = jnp.stack(
        [
            hidden_in.reshape(clip_count, frame_dev, positions, model_width),
            attn_cotangent.reshape(clip_count, frame_dev, positions, model_width),
        ],
        axis=3,
    )
    both = lax.all_to_all(both, "frame", split_axis=2, concat_axis=1, tiled=True)
    frames = both.shape[1]
    across = both.shape[2]
    values_in = both[:, :, :, 0].astype(jnp.float32)
    average = jnp.mean(values_in, axis=-1, keepdims=True)
    centered = values_in - average
    variance = jnp.mean(centered * centered, axis=-1, keepdims=True)
    inverse_std = lax.rsqrt(variance + 1e-06)
    normed = centered * inverse_std
    modulation = modulation_table[timestep].astype(jnp.float32)
    shift = modulation[:, 0][:, None, None, :]
    scale = modulation[:, 1][:, None, None, :]
    modulated = (normed * (1.0 + scale) + shift).astype(jnp.bfloat16)
    mod_rows = modulated.reshape(-1, model_width)
    projected = jnp.dot(mod_rows, w_full, preferred_element_type=jnp.float32).astype(jnp.bfloat16)
    pieces = projected.reshape(clip_count, frames, across, 3, HEADS, HEAD_DIM)
    loss_weight = snr_table[weight_index]
    upstream = (loss_weight[:, None, None, None] * both[:, :, :, 1].astype(jnp.float32)).astype(
        jnp.bfloat16
    )
    upstream = upstream.reshape(clip_count, frames, across, HEADS, HEAD_DIM)
    head_grads = attend_back(pieces[:, :, :, 0], pieces[:, :, :, 1], pieces[:, :, :, 2], upstream)
    grad_rows = jnp.stack(head_grads, axis=3).reshape(-1, 3 * model_width)
    grad_scale_factor = float(mod_rows.shape[0] * frame_n * space_n) ** (-0.5)
    term = lax.dot_general(
        mod_rows, grad_rows, (((0,), (0,)), ((), ())), preferred_element_type=jnp.float32
    ).astype(jnp.bfloat16)
    col_blk = 3 * model_width // frame_n
    share = lax.psum_scatter(term, "space", scatter_dimension=0, tiled=True)
    share = share.reshape(share.shape[0], frame_n, col_blk)
    share = lax.psum_scatter(share, "frame", scatter_dimension=1, tiled=True)
    grad_weight = lax.all_gather(share, "frame", axis=1, tiled=True)
    grad_weight = grad_weight.reshape(share.shape[0], 3 * model_width)
    grad_weight = grad_weight.astype(jnp.float32) * grad_scale_factor
    grad_hidden = lax.dot_general(
        grad_rows, w_full, (((1,), (1,)), ((), ())), preferred_element_type=jnp.float32
    )
    grad_hidden = grad_hidden.reshape(values_in.shape)
    local_sums = jnp.stack(
        [jnp.sum(grad_hidden, axis=(1, 2)), jnp.sum(grad_hidden * normed, axis=(1, 2))], axis=1
    )
    grad_modulation = lax.psum(local_sums, ("frame", "space")) * grad_scale_factor
    grad_normed = grad_hidden * (1.0 + scale)
    grad_input = (
        grad_normed
        - jnp.mean(grad_normed, axis=-1, keepdims=True)
        - normed * jnp.mean(grad_normed * normed, axis=-1, keepdims=True)
    ) * inverse_std
    grad_input = grad_input.astype(jnp.bfloat16)
    grad_input = lax.all_to_all(grad_input, "frame", split_axis=1, concat_axis=2, tiled=True)
    grad_input = grad_input.reshape(clip_count, frame_dev, row_dev, col_count, model_width)
    return (grad_input, grad_weight, grad_modulation)


def solution(mesh):
    in_specs = (
        P(None, "frame", "space", None, None),
        P(None, "frame", "space", None, None),
        P("space", None),
        P(),
        P(),
        P(),
        P(),
    )
    out_specs = (P(None, "frame", "space", None, None), P("space", None), P())
    return jax.shard_map(
        per_device, mesh=mesh, in_specs=in_specs, out_specs=out_specs, check_vma=False
    )
```

profile of v0, /device:TPU:2, one launch (start us, length us, event | category | flops | bytes accessed | tf_op | source)
XLA Modules:
  0.0 375.7 jit_solution(3701805909269728193)
XLA Ops:
  9.6 1.7 copy.39
  11.3 2.7 pad_maximum_fusion.1
  13.9 11.2 %all-to-all-start = ((bf16[2,1,128,2,1152]{4,0,3,1,2:T(2,128)(2,1)}), bf16[2,1,128,2,1152]{4,0,3,1,2:T(2,128)(2,1)S(1)}, u32[]{:S(2)}, u32[]{:S(2)}) async-start(bf16[2,1,128,2,1152]{4,0,3,1,2:T(2,128)(2,1)} %pad_maximum_fusion.1), calls=%async_computation | async-start | bytes 2359296 | tf_op jit(solution)/shard_map/all_to_all | solution.py:47
  25.2 2.9 gather_fusion
  28.9 26.7 %all-to-all-done = bf16[2,1,128,2,1152]{4,0,3,1,2:T(2,128)(2,1)S(1)} async-done(((bf16[2,1,128,2,1152]{4,0,3,1,2:T(2,128)(2,1)}), bf16[2,1,128,2,1152]{4,0,3,1,2:T(2,128)(2,1)S(1)}, u32[]{:S(2)}, u32[]{:S(2)}) %all-to-all-start) | async-done | bytes 1179680 | tf_op jit(solution)/shard_map/all_to_all | solution.py:47
  56.4 3.1 reshape.157
  59.9 28.9 %all-gather.2.cloned.1.call-done = bf16[1152,3456]{1,0:T(8,128)(2,1)} async-done(((bf16[72,3456]{1,0:T(8,128)(2,1)}), bf16[1152,3456]{1,0:T(8,128)(2,1)}) %all-gather.2.cloned.1.call-update) | async-done | bytes 7962640 | tf_op jit(solution)/shard_map/all_gather | solution.py:39
  88.8 7.0 %convolution_convert_fusion.1 = bf16[256,3456]{1,0:T(8,128)(2,1)} fusion(bf16[256,1152]{1,0:T(8,128)(2,1)S(1)} %fusion.8, bf16[1152,3456]{1,0:T(8,128)(2,1)} %all-gather.2.cloned.1.call-done), kind=kOutput, calls=%fused_computation.5 | convolution fusion | flops 2039316480 | bytes 10321920 | tf_op jit(solution)/shard_map/dot_general | solution.py:61
  95.8 7.1 %reshape.152 = bf16[2,16,8,3,16,72]{5,4,3,2,1,0:T(8,128)(2,1)S(1)} reshape(bf16[256,3456]{1,0:T(8,128)(2,1)} %convolution_convert_fusion.1) | data formatting | bytes 3538944 | tf_op jit(solution)/shard_map/reshape | solution.py:62
  103.9 1.7 fusion.4
  105.6 2.3 multiply_reduce_fusion
  107.9 2.4 fusion.6
  110.3 2.2 fusion.7
  112.6 2.8 fusion.5
  116.9 4.6 %dot_general.32 = bf16[2,16,8,3456]{3,2,1,0:T(8,128)(2,1)} reshape(bf16[2,16,8,3,16,72]{5,4,3,2,1,0:T(8,128)(2,1)S(1)} %copy.46) | data formatting | bytes 3538944 | tf_op jit(solution)/shard_map/dot_general | solution.py:81
  121.5 4.6 %reshape.154 = bf16[256,3456]{1,0:T(8,128)(2,1)} reshape(bf16[2,16,8,3,16,72]{5,4,3,2,1,0:T(8,128)(2,1)S(1)} %copy.46) | data formatting | bytes 3538944 | tf_op jit(solution)/shard_map/reshape | solution.py:69
  126.1 6.7 %multiply_reduce_fusion.1 = (f32[2,1152]{1,0:T(2,128)S(1)}, f32[2,16,8]{2,1,0:T(8,128)S(1)}, f32[2,16,8]{2,1,0:T(8,128)S(1)}, f32[2,1152]{1,0:T(2,128)S(1)}, bf1...) fusion(f32[2,16,8]{2,1,0:T(8,128)S(1)} %add_rsqrt_fusion, ...), kind=kOutput, calls=%fused_computation.28 | convolution fusion | flops 2042260480 | bytes 12132352 | tf_op jit(solution)/shard_map/dot_general | solution.py:81
  132.8 5.4 %convolution_convert_fusion = bf16[1152,3456]{1,0:T(8,128)(2,1)} fusion(bf16[256,1152]{1,0:T(8,128)(2,1)S(1)} %bitcast.101, bf16[256,3456]{1,0:T(8,128)(2,1)S(1)} %copy-done.3), kind=kOutput, calls=%fused_computation.2 | convolution fusion | flops 2042413056 | bytes 10321920 | tf_op jit(solution)/shard_map/dot_general | solution.py:71
  140.8 8.8 %all-to-all-start.1 = ((bf16[2,16,8,1152]{3,2,0,1:T(8,128)(2,1)}), bf16[2,16,8,1152]{3,2,0,1:T(8,128)(2,1)S(1)}, u32[]{:S(2)}, u32[]{:S(2)}) async-start(bf16[2,16,8,1152]{3,2,0,1:T(8,128)(2,1)} %copy.47), calls=%async_computation.1 | async-start | bytes 1179648 | tf_op jit(solution)/shard_map/all_to_all | solution.py:96
  149.7 76.9 %reduce-scatter.8.cloned.1.call-done = bf16[72,3456]{1,0:T(8,128)(2,1)} async-done(((bf16[1152,3456]{1,0:T(8,128)(2,1)}), bf16[72,3456]{1,0:T(8,128)(2,1)}) %reduce-scatter.8.cloned.1.call-update) | async-done | bytes 497680
  226.6 2.8 reshape.155
  230.4 80.8 %psum.7 = f32[2,2,1152]{2,0,1:T(2,128)S(1)} all-reduce(f32[2,2,1152]{2,0,1:T(2,128)S(1)} %pad_maximum_fusion.2), channel_id=1, replica_groups=mesh['frame'=16,'space'=16] {'frame','space'}, use_global_device_ids=true, to_apply=%region_10.0 | all-reduce | flops 4608 | bytes 36864 | tf_op jit(solution)/shard_map/psum | solution.py:88
  312.6 8.1 %reduce-scatter.6.cloned.1.call-done = bf16[72,1,216]{2,0,1:T(8,128)(2,1)} async-done(((bf16[72,16,216]{2,0,1:T(8,128)(2,1)}), bf16[72,1,216]{2,0,1:T(8,128)(2,1)}) %reduce-scatter.6.cloned.1.call-update) | async-done | bytes 31120 | tf_op jit(solution)/shard_map/reduce_scatter | solution.py:77
  320.8 46.3 %all_gather.7 = bf16[72,16,216]{2,0,1:T(8,128)(2,1)S(1)} all-gather(bf16[72,1,216]{2,0,1:T(8,128)(2,1)} %reduce-scatter.6.cloned.1.call-done), channel_id=1, replica_groups=mesh['frame'=16,'space'=16] {'frame'}, dimensions={1}, use_global_device_ids=true | all-gather | bytes 528768 | tf_op jit(solution)/shard_map/all_gather | solution.py:78
  (55 shorter events, 14.0 us)
Async XLA Ops:
  7.2 21.0 %copy-start = (f32[1000]{0:T(1024)S(1)}, f32[1000]{0:T(1024)}, u32[]{:S(2)}) copy-start(f32[1000]{0:T(1024)} %param.11) | copy-start | bytes 12004
  7.2 81.6 %all-gather.2.cloned.1.call-start = ((), (), s32[]{:S(2)}) async-start(), calls=%async_computation.4 | async-start | bytes 8460288 | tf_op jit(solution)/shard_map/all_gather | solution.py:39
  11.3 13.9 %copy-start.5 = (s32[2]{0:T(128)S(1)}, s32[2]{0:T(128)}, u32[]{:S(2)}) copy-start(s32[2]{0:T(128)} %param.12) | copy-start | bytes 28
  11.3 16.9 %copy-start.6 = (s32[2]{0:T(128)S(1)}, s32[2]{0:T(128)}, u32[]{:S(2)}) copy-start(s32[2]{0:T(128)} %param.13) | copy-start | bytes 28
  13.9 41.6 %all-to-all-start = ((bf16[2,1,128,2,1152]{4,0,3,1,2:T(2,128)(2,1)}), bf16[2,1,128,2,1152]{4,0,3,1,2:T(2,128)(2,1)S(1)}, u32[]{:S(2)}, u32[]{:S(2)}) async-start(bf16[2,1,128,2,1152]{4,0,3,1,2:T(2,128)(2,1)} %pad_maximum_fusion.1), calls=%async_computation | async-start | bytes 2359296 | tf_op jit(solution)/shard_map/all_to_all | solution.py:47
  25.2 201.4 %reduce-scatter.8.cloned.1.call-start = ((), (), s32[]{:S(2)}) async-start(), calls=%async_computation.6 | async-start | bytes 8460288
  55.7 3.9 %copy-start.1 = (bf16[2,1,128,2,1152]{4,2,0,3,1:T(8,128)(2,1)}, bf16[2,1,128,2,1152]{4,2,0,3,1:T(8,128)(2,1)S(1)}, u32[]{:S(2)}) copy-start(bf16[2,1,128,2,1152]{4,2,0,3,1:T(8,128)(2,1)S(1)} %copy.85) | copy-start | bytes 3538948
  103.9 1.7 copy-start.4
  126.1 6.7 %copy-start.3 = (bf16[256,3456]{1,0:T(8,128)(2,1)S(1)}, bf16[256,3456]{1,0:T(8,128)(2,1)}, u32[]{:S(2)}) copy-start(bf16[256,3456]{1,0:T(8,128)(2,1)} %reshape.154) | copy-start | bytes 5308420
  138.3 1.3 copy-start.2
  140.8 170.9 %all-to-all-start.1 = ((bf16[2,16,8,1152]{3,2,0,1:T(8,128)(2,1)}), bf16[2,16,8,1152]{3,2,0,1:T(8,128)(2,1)S(1)}, u32[]{:S(2)}, u32[]{:S(2)}) async-start(bf16[2,16,8,1152]{3,2,0,1:T(8,128)(2,1)} %copy.47), calls=%async_computation.1 | async-start | bytes 1179648 | tf_op jit(solution)/shard_map/all_to_all | solution.py:96
  149.6 171.1 %reduce-scatter.6.cloned.1.call-start = ((), (), s32[]{:S(2)}) async-start(), calls=%async_computation.5 | async-start | bytes 626688 | tf_op jit(solution)/shard_map/reduce_scatter | solution.py:77
Sparse Core Ops, SparseCore 0:
  9.9 78.8 all-gather.1
  138.4 88.0 reduce-scatter.7
  230.6 90.0 reduce-scatter.5
where the time goes:
time: 376 us
  waiting for transfers between devices  141 us (38%)
  blocking collectives  127 us (34%)
  local copies, waits for them, and re-layouts  37.7 us (10%)
  matrix products  30.6 us (8%)
  starting transfers between devices  20.1 us (5%)
  between operations  14.1 us (4%)
  other arithmetic  4.83 us (1%)
    psum x1, blocking collectives, per_device(): lax.psum(local_sums, ('frame', 'space')) * grad_scale_factor  80.8 us
    unnamed x4, waiting for transfers between devices  77.6 us
    all_gather x1, blocking collectives, per_device(): grad_weight = lax.all_gather(share, 'frame', axis=1, tiled=True)  46.3 us
    all_gather x1, waiting for transfers between devices, per_device(): w_full = lax.all_gather(w_qkv, 'space', axis=0, tiled=True)  28.9 us
    all_to_all x1, waiting for transfers between devices, per_device(): lax.all_to_all(both, 'frame', split_axis=2, concat_axis=1, tiled=True)  26.7 us
    all_to_all x1, starting transfers between devices, per_device(): lax.all_to_all(both, 'frame', split_axis=2, concat_axis=1, tiled=True)  11.2 us
    all_to_all x1, starting transfers between devices, per_device(): lax.all_to_all(grad_input, 'frame', split_axis=1, concat_axis=2, tiled=True)  8.77 us
    reduce_scatter x1, waiting for transfers between devices, per_device(): share = lax.psum_scatter(share, 'frame', scatter_dimension=1, tiled=True)  8.13 us
  transfers between devices with their start and end apart: 5, of which 4 were waited for; matrix products, arithmetic and copies ran while one was open for 5% of the time, Pallas kernels for 0%

commit v1 on v0

--- a/solution.py
+++ b/solution.py
@@ -85,7 +85,9 @@
     local_sums = jnp.stack(
         [jnp.sum(grad_hidden, axis=(1, 2)), jnp.sum(grad_hidden * normed, axis=(1, 2))], axis=1
     )
-    grad_modulation = lax.psum(local_sums, ("frame", "space")) * grad_scale_factor
+    grad_modulation = (
+        jnp.sum(lax.all_gather(local_sums, ("frame", "space")), axis=0) * grad_scale_factor
+    )
     grad_normed = grad_hidden * (1.0 + scale)
     grad_input = (
         grad_normed

time: 376 us -> 792 us (2.11)
  waiting for transfers between devices: 141 us -> 634 us
  blocking collectives: 127 us -> 46.1 us
    all_gather x0 -> x1, waiting for transfers between devices: none -> 418 us  [per_device(): lax.all_gather(local_sums, ('frame', 'space'))]
    psum x1 -> x0, blocking collectives: 80.8 us -> none  [per_device(): lax.psum(local_sums, ('frame', 'space')) * grad_scale_factor]
    reduce_scatter x1, waiting for transfers between devices: 8.13 us -> 83 us  [per_device(): share = lax.psum_scatter(share, 'frame', scatter_dimension=1, tiled=True)]
    unnamed x4 -> x5, waiting for transfers between devices: 77.6 us -> 77.3 us
  transfers between devices with their start and end apart: 5 -> 6, of which waited for: 4 -> 5; matrix products, arithmetic and copies ran while one was open for 5% -> 3% of each run, Pallas kernels for 0% -> 0%
where the time goes in v1:
time: 792 us; the launch traced here: 791 us
  waiting for transfers between devices  634 us (80%)
  blocking collectives  46.1 us (6%)
  local copies, waits for them, and re-layouts  36.4 us (5%)
  matrix products  30.6 us (4%)
  starting transfers between devices  20.4 us (3%)
  between operations  14.1 us (2%)
  other arithmetic  9.72 us (1%)
    all_gather x1, waiting for transfers between devices, per_device(): lax.all_gather(local_sums, ('frame', 'space'))  418 us
    reduce_scatter x1, waiting for transfers between devices, per_device(): share = lax.psum_scatter(share, 'frame', scatter_dimension=1, tiled=True)  83 us
    unnamed x5, waiting for transfers between devices  77.3 us
    all_gather x1, blocking collectives, per_device(): grad_weight = lax.all_gather(share, 'frame', axis=1, tiled=True)  46.1 us
    all_gather x1, waiting for transfers between devices, per_device(): w_full = lax.all_gather(w_qkv, 'space', axis=0, tiled=True)  28.9 us
    all_to_all x1, waiting for transfers between devices, per_device(): lax.all_to_all(both, 'frame', split_axis=2, concat_axis=1, tiled=True)  26.7 us
  transfers between devices with their start and end apart: 6, of which 5 were waited for; matrix products, arithmetic and copies ran while one was open for 3% of the time, Pallas kernels for 0%

profile of v1, /device:TPU:2, one launch (start us, length us, event | category | flops | bytes accessed | tf_op | source)
XLA Modules:
  0.0 791.1 jit_solution(11254931795166205884)
XLA Ops:
  11.3 2.7 pad_maximum_fusion.1
  13.9 11.2 %all-to-all-start = ((bf16[2,1,128,2,1152]{4,0,3,1,2:T(2,128)(2,1)}), bf16[2,1,128,2,1152]{4,0,3,1,2:T(2,128)(2,1)S(1)}, u32[]{:S(2)}, u32[]{:S(2)}) async-start(bf16[2,1,128,2,1152]{4,0,3,1,2:T(2,128)(2,1)} %pad_maximum_fusion.1), calls=%async_computation | async-start | bytes 2359296 | tf_op jit(solution)/shard_map/all_to_all | solution.py:47
  25.2 2.9 gather_fusion
  28.9 26.7 %all-to-all-done = bf16[2,1,128,2,1152]{4,0,3,1,2:T(2,128)(2,1)S(1)} async-done(((bf16[2,1,128,2,1152]{4,0,3,1,2:T(2,128)(2,1)}), bf16[2,1,128,2,1152]{4,0,3,1,2:T(2,128)(2,1)S(1)}, u32[]{:S(2)}, u32[]{:S(2)}) %all-to-all-start) | async-done | bytes 1179680 | tf_op jit(solution)/shard_map/all_to_all | solution.py:47
  56.4 3.1 reshape.157
  59.9 28.9 %all-gather.4.cloned.1.call-done = bf16[1152,3456]{1,0:T(8,128)(2,1)} async-done(((bf16[72,3456]{1,0:T(8,128)(2,1)}), bf16[1152,3456]{1,0:T(8,128)(2,1)}) %all-gather.4.cloned.1.call-update) | async-done | bytes 7962640 | tf_op jit(solution)/shard_map/all_gather | solution.py:39
  88.8 7.0 convolution_convert_fusion.1
  95.8 7.1 reshape.152
  103.9 1.7 fusion.4
  105.6 2.3 multiply_reduce_fusion
  107.9 2.4 fusion.6
  110.4 2.2 fusion.7
  112.6 2.8 fusion.5
  116.9 4.6 dot_general.32
  121.5 4.6 reshape.154
  126.1 6.7 multiply_reduce_fusion.1
  132.8 5.4 convolution_convert_fusion
  140.9 8.8 %all-to-all-start.1 = ((bf16[2,16,8,1152]{3,2,0,1:T(8,128)(2,1)}), bf16[2,16,8,1152]{3,2,0,1:T(8,128)(2,1)S(1)}, u32[]{:S(2)}, u32[]{:S(2)}) async-start(bf16[2,16,8,1152]{3,2,0,1:T(8,128)(2,1)} %copy.45), calls=%async_computation.1 | async-start | bytes 1179648 | tf_op jit(solution)/shard_map/all_to_all | solution.py:98
  149.9 76.6 %reduce-scatter.8.cloned.1.call-done = bf16[72,3456]{1,0:T(8,128)(2,1)} async-done(((bf16[1152,3456]{1,0:T(8,128)(2,1)}), bf16[72,3456]{1,0:T(8,128)(2,1)}) %reduce-scatter.8.cloned.1.call-update) | async-done | bytes 497680
  226.5 2.8 reshape.155
  231.2 417.9 %all-gather.6.cloned.1.call-done = f32[512,2,1152]{2,1,0:T(2,128)} async-done(((f32[2,2,1152]{2,1,0:T(2,128)}), f32[512,2,1152]{2,1,0:T(2,128)}) %all-gather.6.cloned.1.call-update) | async-done | bytes 4718608 | tf_op jit(solution)/shard_map/all_gather | solution.py:89
  649.1 3.7 reduce_sum.89
  653.4 83.0 %reduce-scatter.6.cloned.1.call-done = bf16[72,1,216]{2,0,1:T(8,128)(2,1)} async-done(((bf16[72,16,216]{2,0,1:T(8,128)(2,1)}), bf16[72,1,216]{2,0,1:T(8,128)(2,1)}) %reduce-scatter.6.cloned.1.call-update) | async-done | bytes 31120 | tf_op jit(solution)/shard_map/reduce_scatter | solution.py:77
  736.4 46.1 %all_gather.13 = bf16[72,16,216]{2,0,1:T(8,128)(2,1)S(1)} all-gather(bf16[72,1,216]{2,0,1:T(8,128)(2,1)} %reduce-scatter.6.cloned.1.call-done), channel_id=1, replica_groups=mesh['frame'=16,'space'=16] {'frame'}, dimensions={1}, use_global_device_ids=true | all-gather | bytes 528768 | tf_op jit(solution)/shard_map/all_gather | solution.py:78
  (61 shorter events, 15.9 us)
Async XLA Ops:
  7.2 21.0 %copy-start = (f32[1000]{0:T(1024)S(1)}, f32[1000]{0:T(1024)}, u32[]{:S(2)}) copy-start(f32[1000]{0:T(1024)} %param.11) | copy-start | bytes 12004
  7.2 81.6 %all-gather.4.cloned.1.call-start = ((), (), s32[]{:S(2)}) async-start(), calls=%async_computation.4 | async-start | bytes 8460288 | tf_op jit(solution)/shard_map/all_gather | solution.py:39
  11.3 13.9 %copy-start.6 = (s32[2]{0:T(128)S(1)}, s32[2]{0:T(128)}, u32[]{:S(2)}) copy-start(s32[2]{0:T(128)} %param.12) | copy-start | bytes 28
  11.3 16.9 %copy-start.7 = (s32[2]{0:T(128)S(1)}, s32[2]{0:T(128)}, u32[]{:S(2)}) copy-start(s32[2]{0:T(128)} %param.13) | copy-start | bytes 28
  13.9 41.6 %all-to-all-start = ((bf16[2,1,128,2,1152]{4,0,3,1,2:T(2,128)(2,1)}), bf16[2,1,128,2,1152]{4,0,3,1,2:T(2,128)(2,1)S(1)}, u32[]{:S(2)}, u32[]{:S(2)}) async-start(bf16[2,1,128,2,1152]{4,0,3,1,2:T(2,128)(2,1)} %pad_maximum_fusion.1), calls=%async_computation | async-start | bytes 2359296 | tf_op jit(solution)/shard_map/all_to_all | solution.py:47
  25.2 201.4 %reduce-scatter.8.cloned.1.call-start = ((), (), s32[]{:S(2)}) async-start(), calls=%async_computation.7 | async-start | bytes 8460288
  55.7 3.9 copy-start.2
  103.9 1.7 copy-start.5
  126.1 6.7 copy-start.4
  138.3 1.3 copy-start.3
  138.3 510.8 %all-gather.6.cloned.1.call-start = ((), (), s32[]{:S(2)}) async-start(), calls=%async_computation.6 | async-start | bytes 4737024 | tf_op jit(solution)/shard_map/all_gather | solution.py:89
  140.9 89.5 %all-to-all-start.1 = ((bf16[2,16,8,1152]{3,2,0,1:T(8,128)(2,1)}), bf16[2,16,8,1152]{3,2,0,1:T(8,128)(2,1)S(1)}, u32[]{:S(2)}, u32[]{:S(2)}) async-start(bf16[2,16,8,1152]{3,2,0,1:T(8,128)(2,1)} %copy.45), calls=%async_computation.1 | async-start | bytes 1179648 | tf_op jit(solution)/shard_map/all_to_all | solution.py:98
  149.6 586.7 %reduce-scatter.6.cloned.1.call-start = ((), (), s32[]{:S(2)}) async-start(), calls=%async_computation.5 | async-start | bytes 626688 | tf_op jit(solution)/shard_map/reduce_scatter | solution.py:77
  782.4 2.1 copy-start.1
Sparse Core Ops, SparseCore 0:
  9.9 78.8 all-gather.3
  138.4 88.0 reduce-scatter.7
  229.0 420.0 all-gather.5
  653.0 83.3 reduce-scatter.5
